TPU v7x, 32 devices: a whole 2x2x4 slice. The times are simulated.
32 devices in a mesh: ctx: 8 (over y, x, core), mp: 4 (over z).
Axes of the slice: x: 2, y: 2, z: 4, core: 2. Of those that a mesh axis runs over, the one named last changes fastest.
Arguments:
- tile_embeds: bfloat16 [4, 2048, 768], P('mp', 'ctx'), may hold values from -10 to 10
- norm_gain: float32 [768], replicated, may hold values from 0.1 to 1.9
- norm_bias: float32 [768], replicated, may hold values from -3 to 3
- w_qkv: bfloat16 [768, 2304], P('mp'), may hold values from -1.5 to 1.5
- w_out: bfloat16 [768, 768], P('mp'), may hold values from -0.21875 to 0.21875
- valid_count: int32 [4], P('mp'), may hold values from 256 to 2048
Outputs:
- encoded: bfloat16 [4, 2048, 768], P('mp', 'ctx')
All inputs are finite; a program needn't handle non-finite values.
Results may differ from a plain program's by a relative error of at most 0.008.
The roundings to bfloat16 on the way count: a program that leaves them out, or rounds other values in their place, can miss the bound.
Values may be sent and summed in bfloat16 or wider, within the bound.
No kernel may reach another device: no remote copies, remote signals or barrier semaphores. Data moves between devices by JAX's collectives and lax.ppermute only.
A program may use at most 64 MiB of HBM per device.

v0:
```python
from functools import reduce
import math
import jax
import jax.numpy as jnp
from jax import lax
from jax.sharding import PartitionSpec as P

HEADS = 12
HEAD_DIM = 64
MIDDLE_DILATION = 4
SLIDE_DILATION = 16
SHARDS_PER_SEG = 4
NEG_FILL = -1e30


def as_sent(x):

    def short(part):
        return part.astype(jnp.bfloat16) if part.dtype == jnp.float32 else part

    return jax.tree.map(short, x)


def swapped(value, axis, apart):
    mask = 2**apart
    pairs = [(source, source ^ mask) for source in range(lax.axis_size(axis))]
    return lax.ppermute(value, axis, pairs)


def layer_norm(row_data, norm_gain, norm_bias):
    floats = row_data.astype(jnp.float32)
    centre = jnp.mean(floats, axis=-1, keepdims=True)
    spread = jnp.mean((floats - centre) ** 2, axis=-1, keepdims=True)
    return ((floats - centre) * lax.rsqrt(spread + 1e-05) * norm_gain + norm_bias).astype(
        jnp.bfloat16
    )


def select_rows(head_rows, dilation_rate):
    return jnp.stack(
        [
            head_rows[head_number].reshape(-1, dilation_rate, head_rows.shape[-1])[
                :, head_number % dilation_rate
            ]
            for head_number in range(head_rows.shape[0])
        ]
    )


def build_step(query_block, offsets, dilation_rate, total_valid):
    rescale_factor = 1.0 / math.sqrt(query_block.shape[-1])

    def compute(running, shard_part, first):
        running_max, running_sum, running_num = running
        key_matrix, value_matrix = shard_part
        count_here = key_matrix.shape[1]
        dilated_index = first + jnp.arange(count_here, dtype=jnp.int32)
        key_position = dilated_index[None, :] * dilation_rate + offsets[:, None]
        allowed = key_position < total_valid
        logit_matrix = (
            jnp.einsum("hqe,hke->hqk", query_block, key_matrix, preferred_element_type=jnp.float32)
            * rescale_factor
        )
        logit_matrix = jnp.where(allowed[:, None, :], logit_matrix, NEG_FILL)
        new_max = jnp.maximum(running_max, jnp.max(logit_matrix, axis=-1))
        rescale = jnp.exp(running_max - new_max)
        weights = jnp.where(allowed[:, None, :], jnp.exp(logit_matrix - new_max[..., None]), 0.0)
        running_sum = jnp.sum(weights, axis=-1)
        running_num = jnp.einsum(
            "hqk,hke->hqe",
            weights.astype(jnp.bfloat16),
            value_matrix,
            preferred_element_type=jnp.float32,
        )
        return (new_max, running_sum, running_num)

    return compute


def initial_stats(head_count, query_count, head_dim):
    return (
        jnp.full((head_count, query_count), NEG_FILL, jnp.float32),
        jnp.zeros((head_count, query_count), jnp.float32),
        jnp.zeros((head_count, query_count, head_dim), jnp.float32),
    )


def widen_rows(values, offsets, dilation_rate, fill_value):
    picked = jnp.arange(dilation_rate)[None, :] == offsets[:, None]
    if values.ndim == 2:
        return jnp.where(picked[:, None, :], values[:, :, None], fill_value).reshape(
            values.shape[0], -1
        )
    return jnp.where(picked[:, None, :, None], values[:, :, None, :], fill_value).reshape(
        values.shape[0], -1, values.shape[-1]
    )


def local(tile_embeds, norm_gain, norm_bias, w_qkv, w_out, valid_count):
    tile_rows = tile_embeds[0]
    local_rows = tile_rows.shape[0]
    model_width = tile_rows.shape[1]
    head_count = HEADS
    head_dim = HEAD_DIM
    total_valid = valid_count[0]
    device_index = lax.axis_index("ctx")
    first_row = device_index * local_rows
    normed = layer_norm(tile_rows, norm_gain, norm_bias)
    whole_qkv, whole_out = (
        lax.all_gather(w_qkv, "mp", axis=0, tiled=True),
        lax.all_gather(w_out, "mp", axis=0, tiled=True),
    )
    projected = jnp.dot(normed, whole_qkv, preferred_element_type=jnp.float32).astype(jnp.bfloat16)
    gathered_queries = (
        projected[:, :model_width].reshape(local_rows, head_count, head_dim).transpose(1, 0, 2)
    )
    gathered_keys = (
        projected[:, model_width : 2 * model_width]
        .reshape(local_rows, head_count, head_dim)
        .transpose(1, 0, 2)
    )
    gathered_values = (
        projected[:, 2 * model_width :].reshape(local_rows, head_count, head_dim).transpose(1, 0, 2)
    )
    position = first_row + jnp.arange(local_rows, dtype=jnp.int32)
    key_valid = position < total_valid
    head_shifts = jnp.arange(head_count, dtype=jnp.int32)
    local_step = build_step(gathered_queries, head_shifts * 0, 1, total_valid)
    local_stats = local_step(
        initial_stats(head_count, local_rows, head_dim), (gathered_keys, gathered_values), first_row
    )
    middle_shifts = head_shifts % MIDDLE_DILATION
    middle_queries = select_rows(gathered_queries, MIDDLE_DILATION)
    middle_keys = select_rows(gathered_keys, MIDDLE_DILATION)
    middle_values = select_rows(gathered_values, MIDDLE_DILATION)
    grouped_rows = SHARDS_PER_SEG * local_rows // MIDDLE_DILATION
    mid_step = build_step(middle_queries, middle_shifts, MIDDLE_DILATION, total_valid)
    mid_initial = initial_stats(head_count, middle_queries.shape[1], head_dim)
    gathered = (middle_keys, middle_values)
    for bit_number in range(SHARDS_PER_SEG.bit_length() - 1):
        partner = jax.tree.map(
            lambda part, own: part.astype(own.dtype),
            swapped(as_sent(gathered), "ctx", bit_number),
            gathered,
        )
        lower_half = device_index // (1 << bit_number) % 2 == 0
        gathered = tuple(
            (
                jnp.where(
                    lower_half,
                    jnp.concatenate([own_part, other_part], 1),
                    jnp.concatenate([other_part, own_part], 1),
                )
                for own_part, other_part in zip(gathered, partner)
            )
        )
    middle_state = mid_step(mid_initial, gathered, device_index // SHARDS_PER_SEG * grouped_rows)
    slide_shifts = head_shifts % SLIDE_DILATION
    slide_queries = select_rows(gathered_queries, SLIDE_DILATION)
    slide_keys = select_rows(gathered_keys, SLIDE_DILATION)
    slide_values = select_rows(gathered_values, SLIDE_DILATION)
    slide_step = build_step(slide_queries, slide_shifts, SLIDE_DILATION, total_valid)
    slide_state = slide_step(
        initial_stats(head_count, slide_queries.shape[1], head_dim),
        (
            lax.all_gather(slide_keys, "ctx", axis=1, tiled=True),
            lax.all_gather(slide_values, "ctx", axis=1, tiled=True),
        ),
        jnp.int32(0),
    )
    branches = [local_stats]
    for branch_stats, offsets, dilation_rate in (
        (middle_state, middle_shifts, MIDDLE_DILATION),
        (slide_state, slide_shifts, SLIDE_DILATION),
    ):
        branches.append(
            (
                widen_rows(branch_stats[0], offsets, dilation_rate, NEG_FILL),
                widen_rows(branch_stats[1], offsets, dilation_rate, 0.0),
                widen_rows(branch_stats[2], offsets, dilation_rate, 0.0),
            )
        )
    top_score = reduce(jnp.maximum, [entry[0] for entry in branches])
    denominator = sum((jnp.exp(entry[0] - top_score) * entry[1] for entry in branches))
    weighted_sum = sum((jnp.exp(entry[0] - top_score)[..., None] * entry[2] for entry in branches))
    head_result = jnp.where(key_valid[None, :, None], weighted_sum / denominator[..., None], 0.0)
    attention = head_result.astype(jnp.bfloat16).transpose(1, 0, 2).reshape(local_rows, model_width)
    projection = jnp.dot(attention, whole_out, preferred_element_type=jnp.float32)
    return (tile_rows.astype(jnp.float32) + projection).astype(jnp.bfloat16)[None]


def solution(mesh):
    placed = (P("mp", "ctx", None), P(), P(), P("mp", None), P("mp", None), P("mp"))
    return jax.shard_map(
        local, mesh=mesh, in_specs=placed, out_specs=P("mp", "ctx", None), check_vma=False
    )
```

profile of v0, /device:TPU:0, one launch (start us, length us, event | category | flops | bytes accessed | tf_op | source)
XLA Modules:
  0.0 249.5 jit_solution(8458888001286115925)
XLA Ops:
  13.9 67.7 %all-gather.3.cloned.1.call-done = bf16[768,2304]{1,0:T(8,128)(2,1)} async-done(((bf16[192,2304]{1,0:T(8,128)(2,1)}), bf16[768,2304]{1,0:T(8,128)(2,1)}) %all-gather.3.cloned.1.call-update) | async-done | bytes 3538960 | tf_op jit(solution)/shard_map/all_gather | solution.py:110
  81.7 3.3 %convolution_convert_fusion = bf16[256,2304]{1,0:T(8,128)(2,1)S(1)} fusion(bf16[768,2304]{1,0:T(8,128)(2,1)} %all-gather.3.cloned.1.call-done, bf16[1,256,768]{2,1,0:T(8,128)(2,1)} %param.6, f32[768]{0:T(1024)} %param.8, f32[768]{0:T(1024)} %param.7, f32[256]{0:T(256)S(1)} %add_rsqrt_fusion, f32[256]{0:T(256)S(1)} %broadcast_multiply_fusion), kind=kOutput, calls=%fused_computation | convolution fusion | flops 907739136 | bytes 5120000 | tf_op jit(solution)/shard_map/dot_general | solution.py:113
  104.9 10.6 %all_gather.13 = bf16[12,128,64]{2,1,0:T(8,128)(2,1)S(1)} all-gather(bf16[12,16,64]{2,1,0:T(8,128)(2,1)S(1)} %constant_dynamic-update-slice_fusion.36), channel_id=1, replica_groups=mesh['ctx'=8,'mp'=4] {'ctx'}, dimensions={1}, use_global_device_ids=true | all-gather | bytes 221184 | tf_op jit(solution)/shard_map/all_gather | solution.py:166
  117.5 1.8 fusion
  121.8 1.5 copy.509
  129.2 1.5 slice.560
  133.6 1.5 copy.517
  136.6 1.5 copy.519
  139.5 1.5 copy.521
  142.5 1.5 copy.523
  149.9 1.5 slice.574
  151.3 1.5 copy.529
  154.3 1.5 copy.531
  180.7 10.5 %all_gather.14 = bf16[12,128,64]{2,1,0:T(8,128)(2,1)S(1)} all-gather(bf16[12,16,64]{2,1,0:T(8,128)(2,1)S(1)} %constant_dynamic-update-slice_fusion.60), channel_id=1, replica_groups=mesh['ctx'=8,'mp'=4] {'ctx'}, dimensions={1}, use_global_device_ids=true | all-gather | bytes 221184 | tf_op jit(solution)/shard_map/all_gather | solution.py:167
  204.8 2.1 fusion.1
  207.8 2.1 maximum_select_fusion.4
  214.2 2.7 %copy.559 = f32[12,256,64]{1,2,0:T(8,128)} copy(f32[12,256,64]{2,1,0:T(8,128)} %bitcast.410) | data formatting | bytes 1572864 | tf_op jit(solution)/shard_map/jit(_where)/broadcast_in_dim | solution.py:94
  217.0 1.9 maximum_select_fusion.5
  221.6 2.8 %fusion.78 = (f32[12,64]{1,0:T(8,128)S(1)}, f32[12,64,256]{2,1,0:T(8,128)}) fusion(bf16[12,64,64]{2,1,0:T(8,128)(2,1)} %constant_dynamic-update-slice_fusion, bf16[12,128,64]{2,1,0:T(8,128)(2,1)} %collective-permute-done.1, bf16[12,128,64]{2,1,0:T(8,128)(2,1)} %maximum_select_fusion.4, pred[]{:T(512)S(6)} %eq.109, pred[12,256]{1,0:T(8,128)(4,1)S(1)} %copy-done.12), kind=kOutput, calls=%fused_computation.238 | convolution fusion | flops 27524352 | bytes 1284097 | tf_op jit(solution)/shard_map/hqe,hke->hqk/dot_general | solution.py:61
  226.3 3.9 %collective-permute-done.3 = bf16[12,128,64]{2,1,0:T(8,128)(2,1)} collective-permute-done((bf16[12,128,64]{2,1,0:T(8,128)(2,1)}, bf16[12,128,64]{2,1,0:T(8,128)(2,1)}, u32[]{:S(2)}, u32[]{:S(2)}) %collective-permute-start.3) | collective-permute-done | bytes 196640 | tf_op jit(solution)/shard_map/ppermute | solution.py:27
  230.3 2.1 fusion.40
  233.9 2.7 %copy.534 = f32[12,256,64]{1,2,0:T(8,128)} copy(f32[12,256,64]{2,1,0:T(8,128)} %bitcast.411) | data formatting | bytes 1572864 | tf_op jit(solution)/shard_map/jit(_where)/broadcast_in_dim | solution.py:94
  236.7 3.3 %fusion.26 = bf16[12,256,64]{1,2,0:T(8,128)(2,1)} fusion(bf16[12,256,64]{1,2,0:T(8,128)(2,1)} %bitcast.417, f32[12,256,256]{1,2,0:T(8,128)S(1)} %get-tuple-element.49, f32[12,256]{1,0:T(8,128)} %broadcast_maximum_fusion, pred[256]{0:T(512)(128)(4,1)} %add_compare_fusion.2, f32[12,256,64]{1,2,0:T(8,128)} %copy.559, f32[12,256,64]{1,2,0:T(8,128)} %copy.534, ...), kind=kOutput, calls=%fused_computation.23 | convolution fusion | flops 106561536 | bytes 5572864 | tf_op jit(solution)/shard_map/hqk,hke->hqe/dot_general | solution.py:69
  240.0 2.7 %fusion.17 = bf16[1,256,768]{2,1,0:T(8,128)(2,1)} fusion(bf16[256,768]{0,1:T(8,128)(2,1)} %bitcast.420, bf16[768,768]{1,0:T(8,128)(2,1)} %all-gather.5.cloned.1.call-done, bf16[1,256,768]{2,1,0:T(8,128)(2,1)S(1)} %copy-done), kind=kOutput, calls=%fused_computation.15 | convolution fusion | flops 302579712 | bytes 2359296 | tf_op jit(solution)/shard_map/dot_general | solution.py:188
  (257 shorter events, 100.9 us)
Async XLA Ops:
  6.5 75.1 %all-gather.3.cloned.1.call-start = ((), (), s32[]{:S(2)}) async-start(), calls=%async_computation | async-start | bytes 4423680 | tf_op jit(solution)/shard_map/all_gather | solution.py:110
  7.3 232.8 %all-gather.5.cloned.1.call-start = ((), (), s32[]{:S(2)}) async-start(), calls=%async_computation.1 | async-start | bytes 1474560 | tf_op jit(solution)/shard_map/all_gather | solution.py:111
  13.4 102.5 %copy-start.10 = (pred[12,128]{1,0:T(8,128)(4,1)}, pred[12,128]{1,0:T(8,128)(4,1)S(1)}, u32[]{:S(2)}) copy-start(pred[12,128]{1,0:T(8,128)(4,1)S(1)} %add_compare_fusion.1) | copy-start | bytes 4612
  95.2 112.6 %collective-permute-start = (bf16[12,64,64]{2,1,0:T(8,128)(2,1)}, bf16[12,64,64]{2,1,0:T(8,128)(2,1)}, u32[]{:S(2)}, u32[]{:S(2)}) collective-permute-start(bf16[12,64,64]{2,1,0:T(8,128)(2,1)} %constant_dynamic-update-slice_fusion.12), channel_id=1, source_target_pairs={{0,4},{4,0},{8,12},{12,8},{16,20},{20,16},{24,28},{28,24},{1,5},{5... | collective-permute-start | bytes 294920 | tf_op jit(solution)/shard_map/ppermute | solution.py:27
  95.4 21.5 %copy-start.1 = (bf16[256,768]{0,1:T(8,128)(2,1)}, bf16[256,768]{0,1:T(8,128)(2,1)S(1)}, u32[]{:S(2)}) copy-start(bf16[256,768]{0,1:T(8,128)(2,1)S(1)} %copy.405) | copy-start | bytes 1179652
  121.0 85.9 %copy-start.2 = (bf16[256,768]{0,1:T(8,128)(2,1)}, bf16[256,768]{0,1:T(8,128)(2,1)S(1)}, u32[]{:S(2)}) copy-start(bf16[256,768]{0,1:T(8,128)(2,1)S(1)} %copy.506) | copy-start | bytes 1179652
  155.8 51.1 %copy-start.3 = (f32[12,16,128]{2,1,0:T(8,128)S(1)}, f32[12,16,128]{2,1,0:T(8,128)}, u32[]{:S(2)}) copy-start(f32[12,16,128]{2,1,0:T(8,128)} %get-tuple-element.51) | copy-start | bytes 294916
  155.8 51.1 %copy-start.5 = (f32[12,16]{1,0:T(8,128)S(1)}, f32[12,16]{1,0:T(8,128)}, u32[]{:S(2)}) copy-start(f32[12,16]{1,0:T(8,128)} %broadcast_maximum_fusion.1) | copy-start | bytes 2308
  155.8 51.1 %copy-start.11 = (pred[12,128]{1,0:T(8,128)(4,1)S(1)}, pred[12,128]{1,0:T(8,128)(4,1)}, u32[]{:S(2)}) copy-start(pred[12,128]{1,0:T(8,128)(4,1)} %copy-done.10) | copy-start | bytes 4612
  155.8 51.4 %copy-start.6 = (bf16[64,1,64]{2,1,0:T(2,128)(2,1)S(1)}, bf16[64,1,64]{2,1,0:T(2,128)(2,1)}, u32[]{:S(2)}) copy-start(bf16[64,1,64]{2,1,0:T(2,128)(2,1)} %slice.505) | copy-start | bytes 24580
  170.9 46.1 %collective-permute-start.2 = (bf16[12,64,64]{2,1,0:T(8,128)(2,1)}, bf16[12,64,64]{2,1,0:T(8,128)(2,1)}, u32[]{:S(2)}, u32[]{:S(2)}) collective-permute-start(bf16[12,64,64]{2,1,0:T(8,128)(2,1)} %constant_dynamic-update-slice_fusion.48), channel_id=1, source_target_pairs={{0,4},{4,0},{8,12},{12,8},{16,20},{20,16},{24,28},{28,24},{1,5},{5... | collective-permute-start | bytes 294920 | tf_op jit(solution)/shard_map/ppermute | solution.py:27
  206.9 10.1 %copy-start.4 = (bf16[12,64,64]{2,1,0:T(8,128)(2,1)S(1)}, bf16[12,64,64]{2,1,0:T(8,128)(2,1)}, u32[]{:S(2)}) copy-start(bf16[12,64,64]{2,1,0:T(8,128)(2,1)} %constant_dynamic-update-slice_fusion.48) | copy-start | bytes 294916
  209.9 11.7 %collective-permute-start.1 = (bf16[12,128,64]{2,1,0:T(8,128)(2,1)}, bf16[12,128,64]{2,1,0:T(8,128)(2,1)}, u32[]{:S(2)}, u32[]{:S(2)}) collective-permute-start(bf16[12,128,64]{2,1,0:T(8,128)(2,1)} %maximum_select_fusion.4), channel_id=1, source_target_pairs={{0,8},{4,12},{8,0},{12,4},{16,24},{20,28},{24,16},{28,20},{1,9},{5... | collective-permute-start | bytes 589832 | tf_op jit(solution)/shard_map/ppermute | solution.py:27
  213.0 8.7 %copy-start.12 = (pred[12,256]{1,0:T(8,128)(4,1)S(1)}, pred[12,256]{1,0:T(8,128)(4,1)}, u32[]{:S(2)}) copy-start(pred[12,256]{1,0:T(8,128)(4,1)} %add_compare_fusion) | copy-start | bytes 9220
  218.9 11.4 %collective-permute-start.3 = (bf16[12,128,64]{2,1,0:T(8,128)(2,1)}, bf16[12,128,64]{2,1,0:T(8,128)(2,1)}, u32[]{:S(2)}, u32[]{:S(2)}) collective-permute-start(bf16[12,128,64]{2,1,0:T(8,128)(2,1)} %maximum_select_fusion.5), channel_id=1, source_target_pairs={{0,8},{4,12},{8,0},{12,4},{16,24},{20,28},{24,16},{28,20},{1,9},{5... | collective-permute-start | bytes 589832 | tf_op jit(solution)/shard_map/ppermute | solution.py:27
  232.4 4.2 %copy-start.7 = (f32[12,256]{1,0:T(8,128)S(1)}, f32[12,256]{1,0:T(8,128)}, u32[]{:S(2)}) copy-start(f32[12,256]{1,0:T(8,128)} %fusion.1) | copy-start | bytes 36868
  232.4 4.2 %copy-start.8 = (f32[12,256]{1,0:T(8,128)S(1)}, f32[12,256]{1,0:T(8,128)}, u32[]{:S(2)}) copy-start(f32[12,256]{1,0:T(8,128)} %broadcast_in_dim.281) | copy-start | bytes 36868
  232.4 4.2 %copy-start.9 = (f32[12,256]{1,0:T(8,128)S(1)}, f32[12,256]{1,0:T(8,128)}, u32[]{:S(2)}) copy-start(f32[12,256]{1,0:T(8,128)} %broadcast_in_dim.266) | copy-start | bytes 36868
  232.4 4.2 %copy-start.13 = (pred[12,256]{1,0:T(8,128)(4,1)S(1)}, pred[12,256]{1,0:T(8,128)(4,1)}, u32[]{:S(2)}) copy-start(pred[12,256]{1,0:T(8,128)(4,1)} %copy.456) | copy-start | bytes 9220
  232.4 4.2 %copy-start.14 = (pred[12,256]{1,0:T(8,128)(4,1)S(1)}, pred[12,256]{1,0:T(8,128)(4,1)}, u32[]{:S(2)}) copy-start(pred[12,256]{1,0:T(8,128)(4,1)} %broadcast_in_dim.261) | copy-start | bytes 9220
  236.7 3.3 %copy-start = (bf16[1,256,768]{2,1,0:T(8,128)(2,1)S(1)}, bf16[1,256,768]{2,1,0:T(8,128)(2,1)}, u32[]{:S(2)}) copy-start(bf16[1,256,768]{2,1,0:T(8,128)(2,1)} %param.6) | copy-start | bytes 1179652
Sparse Core Ops, SparseCore 0:
  8.9 72.6 all-gather.2
  83.2 28.6 all-gather.4
where the time goes:
time: 254 us; the launch traced here: 250 us
  local copies, waits for them, and re-layouts  107 us (42%)
  waiting for transfers between devices  74.3 us (29%)
  blocking collectives  21.1 us (8%)
  matrix products  17.2 us (7%)
  between operations  14.9 us (6%)
  other arithmetic  12.8 us (5%)
    all_gather x1, waiting for transfers between devices, local(): lax.all_gather(w_qkv, 'mp', axis=0, tiled=True)  67.7 us
    slice x111, local copies, waits for them, and re-layouts, select_rows(): head_rows[head_number].reshape(-1, dilation_rate, head_rows.shape[-1])  54.9 us
    unnamed x96, local copies, waits for them, and re-layouts  35.4 us
    all_gather x1, blocking collectives, local(): lax.all_gather(slide_keys, 'ctx', axis=1, tiled=True)  10.6 us
    all_gather x1, blocking collectives, local(): lax.all_gather(slide_values, 'ctx', axis=1, tiled=True)  10.5 us
    broadcast_in_dim x4, local copies, waits for them, and re-layouts, widen_rows(): jnp.where(picked[:, None, :, None], values[:, :, None, :], fill_value)  8.16 us
    dot_general x3, matrix products, compute(): jnp.einsum('hqk,hke->hqe', weights.astype(jnp.bfloat16), value_matrix, pr...  5.71 us
    dot_general x3, matrix products, compute(): jnp.einsum('hqe,hke->hqk', query_block, key_matrix, preferred_element_typ...  5.55 us
  transfers between devices with their start and end apart: 6, of which 3 were waited for; matrix products, arithmetic and copies ran while one was open for 54% of the time, Pallas kernels for 0%

commit v1 on v0

--- a/solution.py
+++ b/solution.py
@@ -11,6 +11,16 @@
 SLIDE_DILATION = 16
 SHARDS_PER_SEG = 4
 NEG_FILL = -1e30
+
+
+def ring_gather(x, axis, dim):
+    ways, here, step = (lax.axis_size(axis), lax.axis_index(axis), x.shape[dim])
+    dims = [n * ways if d == dim else n for d, n in enumerate(x.shape)]
+    full = lax.dynamic_update_slice_in_dim(jnp.zeros(dims, x.dtype), x, here * step, axis=dim)
+    for far in range(1, ways):
+        x = lax.ppermute(x, axis, [(d, (d + 1) % ways) for d in range(ways)])
+        full = lax.dynamic_update_slice_in_dim(full, x, (here - far) % ways * step, axis=dim)
+    return full
 
 
 def as_sent(x):
@@ -164,7 +174,7 @@
         initial_stats(head_count, slide_queries.shape[1], head_dim),
         (
             lax.all_gather(slide_keys, "ctx", axis=1, tiled=True),
-            lax.all_gather(slide_values, "ctx", axis=1, tiled=True),
+            ring_gather(slide_values, "ctx", 1),
         ),
         jnp.int32(0),
     )

time: 254 us -> 309 us (1.22)
  the two profiles are of different devices: /device:TPU:0 before, /device:TPU:1 now
where the time goes in v1:
time: 309 us; the launch traced here: 304 us
  local copies, waits for them, and re-layouts  160 us (52%)
  waiting for transfers between devices  70.8 us (23%)
  matrix products  16.6 us (5%)
  starting transfers between devices  16.4 us (5%)
  between operations  15.2 us (5%)
  other arithmetic  13 us (4%)
  blocking collectives  11.9 us (4%)
    all_gather x1, waiting for transfers between devices, local(): lax.all_gather(w_qkv, 'mp', axis=0, tiled=True)  66.3 us
    slice x111, local copies, waits for them, and re-layouts, select_rows(): head_rows[head_number].reshape(-1, dilation_rate, head_rows.shape[-1])  59.2 us
    unnamed x120, local copies, waits for them, and re-layouts  41.2 us
    dynamic_update_slice x7, local copies, waits for them, and re-layouts, ring_gather(): lax.dynamic_update_slice_in_dim(full, x, (here - far) % ways * step, axis...  27 us
    all_gather x1, blocking collectives, local(): lax.all_gather(slide_keys, 'ctx', axis=1, tiled=True)  11.9 us
    ppermute x7, local copies, waits for them, and re-layouts, ring_gather(): x = lax.ppermute(x, axis, [(d, (d + 1) % ways) for d in range(ways)])  10.4 us
    ppermute x7, starting transfers between devices, ring_gather(): x = lax.ppermute(x, axis, [(d, (d + 1) % ways) for d in range(ways)])  9.87 us
    broadcast_in_dim x4, local copies, waits for them, and re-layouts, widen_rows(): jnp.where(picked[:, None, :, None], values[:, :, None, :], fill_value)  8.2 us
  transfers between devices with their start and end apart: 13, of which 4 were waited for; matrix products, arithmetic and copies ran while one was open for 62% of the time, Pallas kernels for 0%

profile of v1, /device:TPU:1, one launch (start us, length us, event | category | flops | bytes accessed | tf_op | source)
XLA Modules:
  0.0 304.1 jit_solution(15619759506395467800)
XLA Ops:
  14.7 66.3 %all-gather.3.cloned.1.call-done = bf16[768,2304]{1,0:T(8,128)(2,1)} async-done(((bf16[192,2304]{1,0:T(8,128)(2,1)}), bf16[768,2304]{1,0:T(8,128)(2,1)}) %all-gather.3.cloned.1.call-update) | async-done | bytes 3538960 | tf_op jit(solution)/shard_map/all_gather | solution.py:120
  81.0 3.3 %convolution_convert_fusion = bf16[256,2304]{1,0:T(8,128)(2,1)S(1)} fusion(bf16[768,2304]{1,0:T(8,128)(2,1)} %all-gather.3.cloned.1.call-done, bf16[1,256,768]{2,1,0:T(8,128)(2,1)} %param.6, f32[768]{0:T(1024)} %param.8, f32[768]{0:T(1024)} %param.7, f32[256]{0:T(256)S(1)} %add_rsqrt_fusion, f32[256]{0:T(256)S(1)} %broadcast_multiply_fusion), kind=kOutput, calls=%fused_computation | convolution fusion | flops 907739136 | bytes 5120000 | tf_op jit(solution)/shard_map/dot_general | solution.py:123
  105.0 11.9 %all_gather.10 = bf16[12,128,64]{2,1,0:T(8,128)(2,1)} all-gather(bf16[12,16,64]{2,1,0:T(8,128)(2,1)S(1)} %constant_dynamic-update-slice_fusion.36), channel_id=1, replica_groups=mesh['ctx'=8,'mp'=4] {'ctx'}, dimensions={1}, use_global_device_ids=true | all-gather | bytes 221184 | tf_op jit(solution)/shard_map/all_gather | solution.py:176
  200.4 2.2 fusion.1
  210.1 2.3 collective-permute-start.6
  213.6 2.3 collective-permute-start.7
  221.6 2.3 collective-permute-start.2
  224.0 4.1 %dynamic_update_slice.24 = bf16[12,128,64]{1,2,0:T(8,128)(2,1)S(1)} dynamic-update-slice(bf16[12,128,64]{1,2,0:T(8,128)(2,1)S(1)} %broadcast_in_dim.278, bf16[12,16,64]{1,2,0:T(8,128)(2,1)} %copy.572, s32[]{:T(128)} %constant.140.clone.1, s32[]{:T(128)S(6)} %select_n.233, s32[]{:T(128)} %constant.140.clone.1) | dynamic-update-slice | bytes 49156 | tf_op jit(solution)/shard_map/dynamic_update_slice | solution.py:19
  229.7 2.5 dynamic_update_slice.25
  233.8 4.1 %dynamic_update_slice.26 = bf16[12,128,64]{1,2,0:T(8,128)(2,1)S(1)} dynamic-update-slice(bf16[12,128,64]{1,2,0:T(8,128)(2,1)S(1)} %dynamic_update_slice.25, bf16[12,16,64]{1,2,0:T(8,128)(2,1)} %copy.574, s32[]{:T(128)} %constant.140.clone.1, s32[]{:T(128)S(6)} %select_n.237, s32[]{:T(128)} %constant.140.clone.1) | dynamic-update-slice | bytes 49156 | tf_op jit(solution)/shard_map/dynamic_update_slice | solution.py:22
  239.5 4.1 %dynamic_update_slice.27 = bf16[12,128,64]{1,2,0:T(8,128)(2,1)S(1)} dynamic-update-slice(bf16[12,128,64]{1,2,0:T(8,128)(2,1)S(1)} %dynamic_update_slice.26, bf16[12,16,64]{1,2,0:T(8,128)(2,1)} %copy.575, s32[]{:T(128)} %constant.140.clone.1, s32[]{:T(128)S(6)} %select_n.239, s32[]{:T(128)} %constant.140.clone.1) | dynamic-update-slice | bytes 49156 | tf_op jit(solution)/shard_map/dynamic_update_slice | solution.py:22
  243.6 2.1 collective-permute-start.9
  245.7 2.1 maximum_select_fusion.4
  249.5 2.1 maximum_select_fusion.5
  251.6 2.2 collective-permute-start.3
  254.7 4.1 %dynamic_update_slice.28 = bf16[12,128,64]{1,2,0:T(8,128)(2,1)S(1)} dynamic-update-slice(bf16[12,128,64]{1,2,0:T(8,128)(2,1)S(1)} %dynamic_update_slice.27, bf16[12,16,64]{1,2,0:T(8,128)(2,1)} %copy.576, s32[]{:T(128)} %constant.140.clone.1, s32[]{:T(128)S(6)} %select_n.241, s32[]{:T(128)} %constant.140.clone.1) | dynamic-update-slice | bytes 49156 | tf_op jit(solution)/shard_map/dynamic_update_slice | solution.py:22
  260.4 4.1 %dynamic_update_slice.29 = bf16[12,128,64]{1,2,0:T(8,128)(2,1)S(1)} dynamic-update-slice(bf16[12,128,64]{1,2,0:T(8,128)(2,1)S(1)} %dynamic_update_slice.28, bf16[12,16,64]{1,2,0:T(8,128)(2,1)} %copy.577, s32[]{:T(128)} %constant.140.clone.1, s32[]{:T(128)S(6)} %select_n.243, s32[]{:T(128)} %constant.140.clone.1) | dynamic-update-slice | bytes 49156 | tf_op jit(solution)/shard_map/dynamic_update_slice | solution.py:22
  266.1 4.1 %dynamic_update_slice.30 = bf16[12,128,64]{1,2,0:T(8,128)(2,1)S(1)} dynamic-update-slice(bf16[12,128,64]{1,2,0:T(8,128)(2,1)S(1)} %dynamic_update_slice.29, bf16[12,16,64]{1,2,0:T(8,128)(2,1)} %copy.578, s32[]{:T(128)} %constant.140.clone.1, s32[]{:T(128)S(6)} %select_n.245, s32[]{:T(128)} %constant.140.clone.1) | dynamic-update-slice | bytes 49156 | tf_op jit(solution)/shard_map/dynamic_update_slice | solution.py:22
  271.8 4.1 %dynamic_update_slice.31 = bf16[12,128,64]{1,2,0:T(8,128)(2,1)S(1)} dynamic-update-slice(bf16[12,128,64]{1,2,0:T(8,128)(2,1)S(1)} %dynamic_update_slice.30, bf16[12,16,64]{1,2,0:T(8,128)(2,1)} %copy.579, s32[]{:T(128)} %constant.140.clone.1, s32[]{:T(128)S(6)} %select_n.247, s32[]{:T(128)} %constant.140.clone.1) | dynamic-update-slice | bytes 49156 | tf_op jit(solution)/shard_map/dynamic_update_slice | solution.py:22
  277.5 2.7 copy.580
  280.2 2.8 fusion.78
  288.5 2.7 copy.548
  291.3 3.3 %fusion.26 = bf16[12,256,64]{1,2,0:T(8,128)(2,1)} fusion(bf16[12,256,64]{1,2,0:T(8,128)(2,1)} %bitcast.415, f32[12,256,256]{1,2,0:T(8,128)S(1)} %get-tuple-element.49, f32[12,256]{1,0:T(8,128)} %broadcast_maximum_fusion, pred[256]{0:T(512)(128)(4,1)} %add_compare_fusion.2, f32[12,256,64]{1,2,0:T(8,128)} %copy.580, f32[12,256,64]{1,2,0:T(8,128)} %copy.548, ...), kind=kOutput, calls=%fused_computation.23 | convolution fusion | flops 106561536 | bytes 5572864 | tf_op jit(solution)/shard_map/hqk,hke->hqe/dot_general | solution.py:79
  294.6 2.7 fusion.17
  (311 shorter events, 144.4 us)
Async XLA Ops:
  6.5 74.5 %all-gather.3.cloned.1.call-start = ((), (), s32[]{:S(2)}) async-start(), calls=%async_computation | async-start | bytes 4423680 | tf_op jit(solution)/shard_map/all_gather | solution.py:120
  7.3 287.4 %all-gather.5.cloned.1.call-start = ((), (), s32[]{:S(2)}) async-start(), calls=%async_computation.1 | async-start | bytes 1474560 | tf_op jit(solution)/shard_map/all_gather | solution.py:121
  94.5 151.1 %collective-permute-start = (bf16[12,64,64]{2,1,0:T(8,128)(2,1)}, bf16[12,64,64]{2,1,0:T(8,128)(2,1)}, u32[]{:S(2)}, u32[]{:S(2)}) collective-permute-start(bf16[12,64,64]{2,1,0:T(8,128)(2,1)} %constant_dynamic-update-slice_fusion.12), channel_id=1, source_target_pairs={{0,4},{4,0},{8,12},{12,8},{16,20},{20,16},{24,28},{28,24},{1,5},{5... | collective-permute-start | bytes 294920 | tf_op jit(solution)/shard_map/ppermute | solution.py:37
  127.6 74.9 %copy-start.2 = (bf16[256,768]{0,1:T(8,128)(2,1)}, bf16[256,768]{0,1:T(8,128)(2,1)S(1)}, u32[]{:S(2)}) copy-start(bf16[256,768]{0,1:T(8,128)(2,1)S(1)} %copy.520) | copy-start | bytes 1179652
  161.0 44.6 %copy-start.12 = (bf16[64,1,64]{2,1,0:T(2,128)(2,1)S(1)}, bf16[64,1,64]{2,1,0:T(2,128)(2,1)}, u32[]{:S(2)}) copy-start(bf16[64,1,64]{2,1,0:T(2,128)(2,1)} %slice.568) | copy-start | bytes 24580
  161.0 45.2 %copy-start.13 = (bf16[64,1,64]{2,1,0:T(2,128)(2,1)S(1)}, bf16[64,1,64]{2,1,0:T(2,128)(2,1)}, u32[]{:S(2)}) copy-start(bf16[64,1,64]{2,1,0:T(2,128)(2,1)} %slice.570) | copy-start | bytes 24580
  161.0 45.8 %copy-start.14 = (bf16[64,1,64]{2,1,0:T(2,128)(2,1)S(1)}, bf16[64,1,64]{2,1,0:T(2,128)(2,1)}, u32[]{:S(2)}) copy-start(bf16[64,1,64]{2,1,0:T(2,128)(2,1)} %slice.572) | copy-start | bytes 24580
  161.0 46.4 %copy-start.3 = (bf16[12,128,64]{2,1,0:T(8,128)(2,1)S(1)}, bf16[12,128,64]{2,1,0:T(8,128)(2,1)}, u32[]{:S(2)}) copy-start(bf16[12,128,64]{2,1,0:T(8,128)(2,1)} %all_gather.10) | copy-start | bytes 589828
  161.0 46.4 %copy-start.21 = (pred[12,128]{1,0:T(8,128)(4,1)S(1)}, pred[12,128]{1,0:T(8,128)(4,1)}, u32[]{:S(2)}) copy-start(pred[12,128]{1,0:T(8,128)(4,1)} %add_compare_fusion.1) | copy-start | bytes 4612
  161.0 46.8 %copy-start.6 = (bf16[64,1,64]{2,1,0:T(2,128)(2,1)S(1)}, bf16[64,1,64]{2,1,0:T(2,128)(2,1)}, u32[]{:S(2)}) copy-start(bf16[64,1,64]{2,1,0:T(2,128)(2,1)} %slice.574) | copy-start | bytes 24580
  161.0 47.4 %copy-start.5 = (bf16[1,256,64]{2,1,0:T(8,128)(2,1)S(1)}, bf16[1,256,64]{2,1,0:T(8,128)(2,1)}, u32[]{:S(2)}) copy-start(bf16[1,256,64]{2,1,0:T(8,128)(2,1)} %copy.543) | copy-start | bytes 98308
  161.1 48.4 %copy-start.4 = (bf16[1,256,64]{2,1,0:T(8,128)(2,1)S(1)}, bf16[1,256,64]{2,1,0:T(8,128)(2,1)}, u32[]{:S(2)}) copy-start(bf16[1,256,64]{2,1,0:T(8,128)(2,1)} %copy.545) | copy-start | bytes 98308
  170.6 45.4 %copy-start.17 = (bf16[12,16,64]{2,1,0:T(8,128)(2,1)}, bf16[12,16,64]{2,1,0:T(8,128)(2,1)S(1)}, u32[]{:S(2)}) copy-start(bf16[12,16,64]{2,1,0:T(8,128)(2,1)S(1)} %constant_dynamic-update-slice_fusion.60) | copy-start | bytes 73732
  170.6 37.9 %collective-permute-start.4 = (bf16[12,16,64]{2,1,0:T(8,128)(2,1)S(1)}, bf16[12,16,64]{2,1,0:T(8,128)(2,1)S(1)}, u32[]{:S(2)}, u32[]{:S(2)}) collective-permute-start(bf16[12,16,64]{2,1,0:T(8,128)(2,1)S(1)} %constant_dynamic-update-slice_fusion.60), channel_id=1, source_target_pairs={{0,4},{4,8},{8,12},{12,16},{16,20},{20,24},{24,28},{28,0},{1,5},{5... | collective-permute-start | bytes 73736 | tf_op jit(solution)/shard_map/ppermute | solution.py:21
  208.5 1.6 collective-permute-start.5
  210.1 3.5 %collective-permute-start.6 = (bf16[12,16,64]{2,1,0:T(8,128)(2,1)S(1)}, bf16[12,16,64]{2,1,0:T(8,128)(2,1)S(1)}, u32[]{:S(2)}, u32[]{:S(2)}) collective-permute-start(bf16[12,16,64]{2,1,0:T(8,128)(2,1)S(1)} %collective-permute-done.5), channel_id=1, source_target_pairs={{0,4},{4,8},{8,12},{12,16},{16,20},{20,24},{24,28},{28,0},{1,5},{5... | collective-permute-start | bytes 73736 | tf_op jit(solution)/shard_map/ppermute | solution.py:21
  213.6 4.4 %collective-permute-start.7 = (bf16[12,16,64]{2,1,0:T(8,128)(2,1)S(1)}, bf16[12,16,64]{2,1,0:T(8,128)(2,1)S(1)}, u32[]{:S(2)}, u32[]{:S(2)}) collective-permute-start(bf16[12,16,64]{2,1,0:T(8,128)(2,1)S(1)} %collective-permute-done.6), channel_id=1, source_target_pairs={{0,4},{4,8},{8,12},{12,16},{16,20},{20,24},{24,28},{28,0},{1,5},{5... | collective-permute-start | bytes 73736 | tf_op jit(solution)/shard_map/ppermute | solution.py:21
  218.0 25.6 %collective-permute-start.8 = (bf16[12,16,64]{2,1,0:T(8,128)(2,1)S(1)}, bf16[12,16,64]{2,1,0:T(8,128)(2,1)}, u32[]{:S(2)}, u32[]{:S(2)}) collective-permute-start(bf16[12,16,64]{2,1,0:T(8,128)(2,1)S(1)} %collective-permute-done.7), channel_id=1, source_target_pairs={{0,4},{4,8},{8,12},{12,16},{16,20},{20,24},{24,28},{28,0},{1,5},{5... | collective-permute-start | bytes 73736 | tf_op jit(solution)/shard_map/ppermute | solution.py:21
  221.6 27.9 %collective-permute-start.2 = (bf16[12,64,64]{2,1,0:T(8,128)(2,1)}, bf16[12,64,64]{2,1,0:T(8,128)(2,1)}, u32[]{:S(2)}, u32[]{:S(2)}) collective-permute-start(bf16[12,64,64]{2,1,0:T(8,128)(2,1)} %constant_dynamic-update-slice_fusion.48), channel_id=1, source_target_pairs={{0,4},{4,0},{8,12},{12,8},{16,20},{20,16},{24,28},{28,24},{1,5},{5... | collective-permute-start | bytes 294920 | tf_op jit(solution)/shard_map/ppermute | solution.py:37
  223.9 52.0 %copy-start.22 = (pred[12,128]{1,0:T(8,128)(4,1)S(1)}, pred[12,128]{1,0:T(8,128)(4,1)}, u32[]{:S(2)}) copy-start(pred[12,128]{1,0:T(8,128)(4,1)} %add_compare_fusion.1) | copy-start | bytes 4612
  243.6 5.5 %collective-permute-start.9 = (bf16[12,16,64]{2,1,0:T(8,128)(2,1)}, bf16[12,16,64]{2,1,0:T(8,128)(2,1)}, u32[]{:S(2)}, u32[]{:S(2)}) collective-permute-start(bf16[12,16,64]{2,1,0:T(8,128)(2,1)} %collective-permute-done.8), channel_id=1, source_target_pairs={{0,4},{4,8},{8,12},{12,16},{16,20},{20,24},{24,28},{28,0},{1,5},{5... | collective-permute-start | bytes 73736 | tf_op jit(solution)/shard_map/ppermute | solution.py:21
  247.8 32.4 %collective-permute-start.1 = (bf16[12,128,64]{2,1,0:T(8,128)(2,1)}, bf16[12,128,64]{2,1,0:T(8,128)(2,1)}, u32[]{:S(2)}, u32[]{:S(2)}) collective-permute-start(bf16[12,128,64]{2,1,0:T(8,128)(2,1)} %maximum_select_fusion.4), channel_id=1, source_target_pairs={{0,8},{4,12},{8,0},{12,4},{16,24},{20,28},{24,16},{28,20},{1,9},{5... | collective-permute-start | bytes 589832 | tf_op jit(solution)/shard_map/ppermute | solution.py:37
  249.0 21.2 %collective-permute-start.10 = (bf16[12,16,64]{2,1,0:T(8,128)(2,1)}, bf16[12,16,64]{2,1,0:T(8,128)(2,1)}, u32[]{:S(2)}, u32[]{:S(2)}) collective-permute-start(bf16[12,16,64]{2,1,0:T(8,128)(2,1)} %collective-permute-done.9), channel_id=1, source_target_pairs={{0,4},{4,8},{8,12},{12,16},{16,20},{20,24},{24,28},{28,0},{1,5},{5... | collective-permute-start | bytes 73736 | tf_op jit(solution)/shard_map/ppermute | solution.py:21
  251.6 33.2 %collective-permute-start.3 = (bf16[12,128,64]{2,1,0:T(8,128)(2,1)}, bf16[12,128,64]{2,1,0:T(8,128)(2,1)}, u32[]{:S(2)}, u32[]{:S(2)}) collective-permute-start(bf16[12,128,64]{2,1,0:T(8,128)(2,1)} %maximum_select_fusion.5), channel_id=1, source_target_pairs={{0,8},{4,12},{8,0},{12,4},{16,24},{20,28},{24,16},{28,20},{1,9},{5... | collective-permute-start | bytes 589832 | tf_op jit(solution)/shard_map/ppermute | solution.py:37
  (16 other events, 313.6 us)
Sparse Core Ops, SparseCore 0:
  8.9 72.0 all-gather.2
  82.6 28.4 all-gather.4
